TPU v7x, 256 devices: a whole 4x4x8 slice. The times are simulated.
256 devices in a mesh: req: 64 (over y, z, core), tp: 4 (over x).
Axes of the slice: x: 4, y: 4, z: 8, core: 2. Of those that a mesh axis runs over, the one named last changes fastest.
Arguments:
- patches: bfloat16 [16384, 1280], P('req'), may hold values from -6 to 6
- half_grid: int32 [64, 2], P('req'), may hold values from 6 to 8
- text_embed: bfloat16 [12288, 1280], P('req'), may hold values from -6 to 6
- dest_dev: int32 [4096], P('req'), may hold values from 0 to 63, as said below
- dest_pos: int32 [4096], P('req'), may hold values from 0 to 191, as said below
- text_len: int32 [64], P('req'), may hold values from 1 to 128, as said below
- enc_qkv: bfloat16 [1280, 3840], P('req', 'tp')
- enc_out_t: bfloat16 [1280, 1280], P('req', 'tp'), may hold values from -0.15625 to 0.15625
- enc_up: bfloat16 [1280, 5120], P('req', 'tp'), may hold values from -0.15625 to 0.15625
- enc_down_t: bfloat16 [1280, 5120], P('req', 'tp'), may hold values from -0.078125 to 0.078125
- merge_t: bfloat16 [1280, 5120], P('req', 'tp'), may hold values from -0.078125 to 0.078125
- dec_qkv: bfloat16 [1280, 3840], P('req', 'tp')
- dec_out_t: bfloat16 [1280, 1280], P('req', 'tp'), may hold values from -0.15625 to 0.15625
- dec_up: bfloat16 [1280, 5120], P('req', 'tp'), may hold values from -0.15625 to 0.15625
- dec_down_t: bfloat16 [1280, 5120], P('req', 'tp'), may hold values from -0.078125 to 0.078125
Outputs:
- decoded: bfloat16 [12288, 1280], P('req')
Inputs may be any that keep to these rules, and one draw needn't show every extreme that they name: `dest_dev`: the slots of one device go in runs to destination devices; at most 2 slots of one device name one destination device, exactly 2 for some pairs; every device is named by exactly 64 slots in all. `dest_pos`: positions named for one destination device are distinct and below 64 plus its text_len. `text_len`: some request has exactly 128.
All inputs are finite; a program needn't handle non-finite values.
Results may differ from a plain program's by a relative error of at most 0.024.
Values may be sent and summed in bfloat16 or wider, within the bound.
A program may use at most 64 MiB of HBM per device.

v0:
```python
import jax
import jax.numpy as jnp
from jax import lax
from jax.sharding import PartitionSpec as P

HEAD_DIM = 80
GRID = 16
EPS = 1e-06


def for_sending(shard):

    def short(part):
        return part.astype(jnp.bfloat16) if part.dtype == jnp.float32 else part

    return jax.tree.map(short, shard)


def normalize(stream):
    values_f = stream.astype(jnp.float32)
    center = values_f - jnp.mean(values_f, axis=-1, keepdims=True)
    spread = jnp.mean(center * center, axis=-1, keepdims=True)
    return (center * lax.rsqrt(spread + EPS)).astype(jnp.bfloat16)


def fetch_weights(weights):
    return jax.tree.map(
        lambda part, own: part.astype(own.dtype),
        lax.all_gather(for_sending(weights), "req", axis=0, tiled=True),
        weights,
    )


def tensor_total(partial_value):
    return lax.psum(partial_value.astype(jnp.bfloat16), "tp").astype(jnp.float32)


def attention(normed, w_qkv, w_out_t, allowed, sample_count):
    total_rows = normed.shape[0]
    length = total_rows // sample_count
    projected = jnp.dot(normed, w_qkv, preferred_element_type=jnp.float32).astype(jnp.bfloat16)
    projected = projected.reshape(sample_count, length, -1, 3, HEAD_DIM)
    queries = projected[:, :, :, 0]
    key_part = projected[:, :, :, 1]
    value_part = projected[:, :, :, 2]
    scores = jnp.einsum(
        "bqhd,bkhd->bhqk", queries, key_part, preferred_element_type=jnp.float32
    ) * HEAD_DIM ** (-0.5)
    scores = jnp.where(allowed, scores, -1e30)
    highest = jnp.max(scores, axis=-1, keepdims=True)
    exponent = jnp.exp(scores - highest)
    weights_soft = (exponent / jnp.sum(exponent, axis=-1, keepdims=True)).astype(jnp.bfloat16)
    heads_out = jnp.einsum(
        "bhqk,bkhd->bqhd", weights_soft, value_part, preferred_element_type=jnp.float32
    )
    heads_out = heads_out.astype(jnp.bfloat16).reshape(total_rows, -1)
    return lax.dot_general(
        heads_out, w_out_t, (((1,), (1,)), ((), ())), preferred_element_type=jnp.float32
    )


def feed_forward(normed, w_up, w_down_t):
    hidden = jax.nn.gelu(
        jnp.dot(normed, w_up, preferred_element_type=jnp.float32), approximate=False
    )
    hidden = hidden.astype(jnp.bfloat16)
    return lax.dot_general(
        hidden, w_down_t, (((1,), (1,)), ((), ())), preferred_element_type=jnp.float32
    )


def transformer_layer(stream, weights, allowed, sample_count):
    w_qkv, w_out_t, w_up, w_down_t = weights
    attended = attention(normalize(stream), w_qkv, w_out_t, allowed, sample_count)
    middle = (stream.astype(jnp.float32) + tensor_total(attended)).astype(jnp.bfloat16)
    result_rows = middle.astype(jnp.float32) + tensor_total(
        feed_forward(normalize(middle), w_up, w_down_t)
    )
    result_rows = result_rows.astype(jnp.bfloat16)
    return result_rows


def on_device(
    patches,
    half_grid,
    text_embed,
    dest_dev,
    dest_pos,
    text_len,
    enc_qkv,
    enc_out_t,
    enc_up,
    enc_down_t,
    merge_t,
    dec_qkv,
    dec_out_t,
    dec_up,
    dec_down_t,
):
    image_count = half_grid.shape[0]
    model_width = patches.shape[1]
    per_image = GRID * GRID
    patch_index = jnp.arange(per_image, dtype=jnp.int32)
    key_valid = ((patch_index // GRID)[None, :] < 2 * half_grid[:, 0:1]) & (
        (patch_index % GRID)[None, :] < 2 * half_grid[:, 1:2]
    )
    enc_weights = fetch_weights((enc_qkv, enc_out_t, enc_up, enc_down_t))
    encoded = transformer_layer(patches, enc_weights, key_valid[:, None, None, :], image_count)
    merge_local, qkv_dec, out_dec, up_dec, down_dec = fetch_weights(
        (merge_t, dec_qkv, dec_out_t, dec_up, dec_down_t)
    )
    half_side = GRID // 2
    blocks = encoded.reshape(image_count, half_side, 2, half_side, 2, model_width).transpose(
        0, 1, 3, 2, 4, 5
    )
    blocks = blocks.reshape(image_count * half_side * half_side, 4 * model_width)
    span_width = merge_local.shape[1]
    feature_part = lax.dynamic_slice_in_dim(
        blocks, lax.axis_index("tp") * span_width, span_width, 1
    )
    merge_partial = lax.dot_general(
        feature_part, merge_local, (((1,), (1,)), ((), ())), preferred_element_type=jnp.float32
    )
    merged = tensor_total(merge_partial).astype(jnp.bfloat16)
    slot_count = merged.shape[0]
    senders = lax.axis_size("req")
    even_share = slot_count // senders
    capacity = even_share + max(even_share // 2, 1)
    cell_index = jnp.arange(half_side * half_side, dtype=jnp.int32)
    slot_valid = ((cell_index // half_side)[None, :] < half_grid[:, 0:1]) & (
        (cell_index % half_side)[None, :] < half_grid[:, 1:2]
    )
    slot_valid = slot_valid.reshape(slot_count)
    one_hot = (dest_dev[:, None] == jnp.arange(senders, dtype=jnp.int32)[None, :]).astype(jnp.int32)
    earlier = jnp.cumsum(one_hot, axis=0) - one_hot
    slot_rank = jnp.sum(earlier * one_hot, axis=1)
    outgoing = (
        jnp.zeros((senders, capacity, model_width), jnp.bfloat16)
        .at[dest_dev, slot_rank]
        .set(merged)
    )
    out_pos = (
        jnp.full((senders, capacity), -1, jnp.int32)
        .at[dest_dev, slot_rank]
        .set(jnp.where(slot_valid, dest_pos, -1))
    )
    incoming, in_pos = (
        lax.all_to_all(outgoing, "req", split_axis=0, concat_axis=0, tiled=True),
        lax.all_to_all(out_pos, "req", split_axis=0, concat_axis=0, tiled=True),
    )
    seq_len = text_embed.shape[0]
    target = jnp.where(in_pos >= 0, in_pos, seq_len).astype(jnp.int32).reshape(-1)
    dec_input = text_embed.at[target].set(incoming.reshape(-1, model_width), mode="drop")
    positions = jnp.arange(seq_len, dtype=jnp.int32)
    causal = (positions[:, None] >= positions[None, :])[None, None]
    decoded = transformer_layer(dec_input, (qkv_dec, out_dec, up_dec, down_dec), causal, 1)
    keep_mask = positions < slot_count + text_len[0]
    return jnp.where(keep_mask[:, None], decoded, jnp.zeros_like(decoded))


def solution(mesh):
    return jax.shard_map(
        on_device,
        mesh=mesh,
        in_specs=(
            P("req", None),
            P("req", None),
            P("req", None),
            P("req"),
            P("req"),
            P("req"),
            P("req", "tp"),
            P("req", "tp"),
            P("req", "tp"),
            P("req", "tp"),
            P("req", "tp"),
            P("req", "tp"),
            P("req", "tp"),
            P("req", "tp"),
            P("req", "tp"),
        ),
        out_specs=P("req", None),
        check_vma=False,
    )
```

profile of v0, /device:TPU:8, one launch (start us, length us, event | category | flops | bytes accessed | tf_op | source)
XLA Modules:
  0.0 852.3 jit_solution(17187715245024345156)
XLA Ops:
  6.5 0.7 all-gather.17.cloned.1.call-update
  7.3 1.4 fusion.214
  10.0 53.3 %all-gather.1 = bf16[64,20,320]{2,1,0:T(8,128)(2,1)S(1)} all-gather(bf16[1,20,320]{2,1,0:T(8,128)(2,1)} %bitcast.120), channel_id=1, replica_groups=mesh['req'=64,'tp'=4] {'req'}, dimensions={0}, use_global_device_ids=true | all-gather | bytes 832000 | tf_op jit(solution)/shard_map/all_gather | solution.py:29
  63.3 0.4 reshape.279
  63.7 0.6 copy-done.1
  64.6 0.3 fusion.12
  64.9 25.2 %all-gather.17.cloned.1.call-done = bf16[64,20,960]{2,1,0:T(8,128)(2,1)} async-done(((bf16[1,20,960]{2,1,0:T(8,128)(2,1)}), bf16[64,20,960]{2,1,0:T(8,128)(2,1)}) %all-gather.17.cloned.1.call-update) | async-done | bytes 2457616 | tf_op jit(solution)/shard_map/all_gather | solution.py:29
  90.1 5.5 reshape.277
  95.6 2.9 convolution_convert_fusion.5
  98.5 0.3 fusion.9
  98.9 0.5 fusion.215
  99.4 0.4 convolution_convert_fusion.8
  99.8 1.4 convolution_convert_fusion
  101.3 0.7 all-gather.19.cloned.1.call-update
  102.1 0.5 all-gather.21.cloned.1.call-update
  102.6 0.5 all-gather.23.cloned.1.call-update
  103.2 45.6 %all-reduce.6.cloned.1.call-done = bf16[256,1280]{1,0:T(8,128)(2,1)} async-done(((bf16[256,1280]{1,0:T(8,128)(2,1)}), bf16[256,1280]{1,0:T(8,128)(2,1)}) %all-reduce.6.cloned.1.call-update) | async-done | bytes 655376 | tf_op jit(solution)/shard_map/psum | solution.py:35
  148.8 1.4 convert_reduce_fusion
  150.5 79.6 %all-gather.19.cloned.1.call-done = bf16[64,20,1280]{2,1,0:T(8,128)(2,1)} async-done(((bf16[1,20,1280]{2,1,0:T(8,128)(2,1)}), bf16[64,20,1280]{2,1,0:T(8,128)(2,1)}) %all-gather.19.cloned.1.call-update) | async-done | bytes 3276816 | tf_op jit(solution)/shard_map/all_gather | solution.py:29
  230.1 6.1 reshape.281
  236.2 72.5 %all-gather.21.cloned.1.call-done = bf16[64,20,1280]{2,1,0:T(8,128)(2,1)} async-done(((bf16[1,20,1280]{2,1,0:T(8,128)(2,1)}), bf16[64,20,1280]{2,1,0:T(8,128)(2,1)}) %all-gather.21.cloned.1.call-update) | async-done | bytes 3276816 | tf_op jit(solution)/shard_map/all_gather | solution.py:29
  308.7 6.1 reshape.283
  314.8 8.2 convolution_convert_fusion.1
  323.3 64.0 %all-gather.23.cloned.1.call-done = bf16[64,20,1280]{2,1,0:T(8,128)(2,1)} async-done(((bf16[1,20,1280]{2,1,0:T(8,128)(2,1)}), bf16[64,20,1280]{2,1,0:T(8,128)(2,1)}) %all-gather.23.cloned.1.call-update) | async-done | bytes 3276816 | tf_op jit(solution)/shard_map/all_gather | solution.py:29
  387.3 4.6 reshape.285
  391.9 44.6 %all-reduce.8.cloned.1.call-done = bf16[256,1280]{1,0:T(8,128)(2,1)} async-done(((bf16[256,1280]{1,0:T(8,128)(2,1)}), bf16[256,1280]{1,0:T(8,128)(2,1)}) %all-reduce.8.cloned.1.call-update) | async-done | bytes 655376 | tf_op jit(solution)/shard_map/psum | solution.py:35
  436.5 2.3 fusion.15
  438.8 2.6 reshape.248
  441.4 2.4 copy.56
  443.8 2.9 reshape.249
  446.7 2.7 convolution_convert_fusion.4
  449.5 0.7 all-gather.25.cloned.1.call-update
  450.3 0.7 all-gather.27.cloned.1.call-update
  451.0 0.5 all-gather.29.cloned.1.call-update
  451.9 1.3 and_select_fusion.2
  453.2 3.5 scatter_fusion
  456.7 0.7 copy.36
  457.4 10.6 %all-to-all-start = ((s32[64,1,2]{2,1,0:T(1,128)}), s32[64,1,2]{2,1,0:T(1,128)S(1)}, u32[]{:S(2)}, u32[]{:S(2)}) async-start(s32[64,1,2]{2,1,0:T(1,128)} %copy.36), calls=%async_computation | async-start | bytes 65536 | tf_op jit(solution)/shard_map/all_to_all | solution.py:149
  468.0 28.8 %all-reduce.10.cloned.1.call-done = bf16[64,1280]{1,0:T(8,128)(2,1)} async-done(((bf16[64,1280]{1,0:T(8,128)(2,1)}), bf16[64,1280]{1,0:T(8,128)(2,1)}) %all-reduce.10.cloned.1.call-update) | async-done | bytes 163856 | tf_op jit(solution)/shard_map/psum | solution.py:35
  496.8 0.9 broadcast_in_dim.47
  497.7 10.0 %scatter_fusion.1 = bf16[64,2,1280]{2,1,0:T(2,128)(2,1)} fusion(bf16[64,2,1280]{2,1,0:T(2,128)(2,1)} %broadcast_in_dim.47, s32[64]{0:T(128)S(1)} %fusion.146, bf16[64,1280]{1,0:T(8,128)(2,1)} %all-reduce.10.cloned.1.call-done), kind=kCustom, calls=%fused_computation.1 | custom fusion | bytes 492032 | tf_op jit(solution)/shard_map/scatter | solution.py:140
  507.7 10.6 %all-to-all-start.1 = ((bf16[64,2,1280]{2,1,0:T(2,128)(2,1)}), bf16[64,2,1280]{2,1,0:T(2,128)(2,1)S(1)}, u32[]{:S(2)}, u32[]{:S(2)}) async-start(bf16[64,2,1280]{2,1,0:T(2,128)(2,1)} %scatter_fusion.1), calls=%async_computation.1 | async-start | bytes 655360 | tf_op jit(solution)/shard_map/all_to_all | solution.py:148
  518.4 54.4 %all-gather.6 = bf16[64,20,320]{2,1,0:T(8,128)(2,1)S(1)} all-gather(bf16[1,20,320]{2,1,0:T(8,128)(2,1)S(1)} %bitcast.121), channel_id=1, replica_groups=mesh['req'=64,'tp'=4] {'req'}, dimensions={0}, use_global_device_ids=true | all-gather | bytes 832000 | tf_op jit(solution)/shard_map/all_gather | solution.py:29
  572.8 0.4 reshape.289
  573.3 0.5 broadcast.367
  573.8 0.6 reduce.11
  574.5 4.0 all-gather.25.cloned.1.call-done
  578.5 5.5 reshape.287
  584.2 0.9 copy-done
  585.1 1.6 scatter_fusion.2
  587.1 2.5 convolution_convert_fusion.6
  589.8 0.5 fusion.216
  590.3 0.3 fusion.27
  590.6 0.3 convolution_convert_fusion.7
  590.9 1.3 convolution_convert_fusion.3
  592.3 65.9 %all-gather.27.cloned.1.call-done = bf16[64,20,1280]{2,1,0:T(8,128)(2,1)} async-done(((bf16[1,20,1280]{2,1,0:T(8,128)(2,1)}), bf16[64,20,1280]{2,1,0:T(8,128)(2,1)}) %all-gather.27.cloned.1.call-update) | async-done | bytes 3276816 | tf_op jit(solution)/shard_map/all_gather | solution.py:29
  658.2 6.1 reshape.291
  664.3 72.8 %all-gather.29.cloned.1.call-done = bf16[64,20,1280]{2,1,0:T(8,128)(2,1)} async-done(((bf16[1,20,1280]{2,1,0:T(8,128)(2,1)}), bf16[64,20,1280]{2,1,0:T(8,128)(2,1)}) %all-gather.29.cloned.1.call-update) | async-done | bytes 3276816 | tf_op jit(solution)/shard_map/all_gather | solution.py:29
  737.1 6.1 reshape.293
  743.2 42.6 %all-reduce.12.cloned.1.call-done = bf16[192,1280]{1,0:T(8,128)(2,1)} async-done(((bf16[192,1280]{1,0:T(8,128)(2,1)}), bf16[192,1280]{1,0:T(8,128)(2,1)}) %all-reduce.12.cloned.1.call-update) | async-done | bytes 491536 | tf_op jit(solution)/shard_map/psum | solution.py:35
  785.8 1.3 convert_reduce_fusion.2
  787.4 7.4 convolution_convert_fusion.2
  795.5 48.0 %all-reduce.14.cloned.1.call-done = bf16[192,1280]{1,0:T(8,128)(2,1)} async-done(((bf16[192,1280]{1,0:T(8,128)(2,1)}), bf16[192,1280]{1,0:T(8,128)(2,1)}) %all-reduce.14.cloned.1.call-update) | async-done | bytes 491536 | tf_op jit(solution)/shard_map/psum | solution.py:35
  843.5 2.0 fusion.93
  (54 shorter events, 2.8 us)
Async XLA Ops:
  6.5 83.6 %all-gather.17.cloned.1.call-start = ((), (), s32[]{:S(2)}) async-start(), calls=%async_computation.7 | async-start | bytes 3194880 | tf_op jit(solution)/shard_map/all_gather | solution.py:29
  7.3 141.5 %all-reduce.6.cloned.1.call-start = ((), (), s32[]{:S(2)}) async-start(), calls=%async_computation.2 | async-start | bytes 1310720 | tf_op jit(solution)/shard_map/psum | solution.py:35
  63.3 1.1 copy-start.1
  101.3 128.8 %all-gather.19.cloned.1.call-start = ((), (), s32[]{:S(2)}) async-start(), calls=%async_computation.8 | async-start | bytes 3993600 | tf_op jit(solution)/shard_map/all_gather | solution.py:29
  102.0 206.7 %all-gather.21.cloned.1.call-start = ((), (), s32[]{:S(2)}) async-start(), calls=%async_computation.9 | async-start | bytes 3993600 | tf_op jit(solution)/shard_map/all_gather | solution.py:29
  102.6 284.7 %all-gather.23.cloned.1.call-start = ((), (), s32[]{:S(2)}) async-start(), calls=%async_computation.10 | async-start | bytes 3993600 | tf_op jit(solution)/shard_map/all_gather | solution.py:29
  103.2 333.4 %all-reduce.8.cloned.1.call-start = ((), (), s32[]{:S(2)}) async-start(), calls=%async_computation.3 | async-start | bytes 1310720 | tf_op jit(solution)/shard_map/psum | solution.py:35
  150.1 164.6 %copy-start.2 = (bf16[256,1280]{1,0:T(8,128)(2,1)}, bf16[256,1280]{1,0:T(8,128)(2,1)S(1)}, u32[]{:S(2)}) copy-start(bf16[256,1280]{1,0:T(8,128)(2,1)S(1)} %get-tuple-element.8) | copy-start | bytes 1966084
  323.0 173.8 %all-reduce.10.cloned.1.call-start = ((), (), s32[]{:S(2)}) async-start(), calls=%async_computation.4 | async-start | bytes 327680 | tf_op jit(solution)/shard_map/psum | solution.py:35
  446.7 4.8 copy-start.4
  446.7 5.2 copy-start.5
  449.5 129.1 %all-gather.25.cloned.1.call-start = ((), (), s32[]{:S(2)}) async-start(), calls=%async_computation.11 | async-start | bytes 3194880 | tf_op jit(solution)/shard_map/all_gather | solution.py:29
  450.2 208.0 %all-gather.27.cloned.1.call-start = ((), (), s32[]{:S(2)}) async-start(), calls=%async_computation.12 | async-start | bytes 3993600 | tf_op jit(solution)/shard_map/all_gather | solution.py:29
  451.0 286.2 %all-gather.29.cloned.1.call-start = ((), (), s32[]{:S(2)}) async-start(), calls=%async_computation.13 | async-start | bytes 3993600 | tf_op jit(solution)/shard_map/all_gather | solution.py:29
  457.4 50.3 %all-to-all-start = ((s32[64,1,2]{2,1,0:T(1,128)}), s32[64,1,2]{2,1,0:T(1,128)S(1)}, u32[]{:S(2)}, u32[]{:S(2)}) async-start(s32[64,1,2]{2,1,0:T(1,128)} %copy.36), calls=%async_computation | async-start | bytes 65536 | tf_op jit(solution)/shard_map/all_to_all | solution.py:149
  497.7 20.6 %copy-start.3 = (bf16[20,320]{1,0:T(8,128)(2,1)S(1)}, bf16[20,320]{1,0:T(8,128)(2,1)}, u32[]{:S(2)}) copy-start(bf16[20,320]{1,0:T(8,128)(2,1)} %param.27) | copy-start | bytes 38404
  507.7 76.3 %all-to-all-start.1 = ((bf16[64,2,1280]{2,1,0:T(2,128)(2,1)}), bf16[64,2,1280]{2,1,0:T(2,128)(2,1)S(1)}, u32[]{:S(2)}, u32[]{:S(2)}) async-start(bf16[64,2,1280]{2,1,0:T(2,128)(2,1)} %scatter_fusion.1), calls=%async_computation.1 | async-start | bytes 655360 | tf_op jit(solution)/shard_map/all_to_all | solution.py:148
  518.3 267.5 %all-reduce.12.cloned.1.call-start = ((), (), s32[]{:S(2)}) async-start(), calls=%async_computation.5 | async-start | bytes 983040 | tf_op jit(solution)/shard_map/psum | solution.py:35
  584.0 1.0 copy-start
  592.3 251.2 %all-reduce.14.cloned.1.call-start = ((), (), s32[]{:S(2)}) async-start(), calls=%async_computation.6 | async-start | bytes 983040 | tf_op jit(solution)/shard_map/psum | solution.py:35
Sparse Core Ops, SparseCore 0:
  10.1 79.9 all-gather.16
  101.4 47.3 all-reduce.5
  151.5 78.5 all-gather.18
  232.6 76.0 all-gather.20
  311.2 76.0 all-gather.22
  389.5 47.0 all-reduce.7
  449.6 47.2 all-reduce.9
  500.0 78.5 all-gather.24
  581.6 76.5 all-gather.26
  661.1 76.0 all-gather.28
  739.6 46.1 all-reduce.11
  794.9 48.4 all-reduce.13
where the time goes:
time: 854 us; the launch traced here: 852 us
  waiting for transfers between devices  598 us (70%)
  blocking collectives  108 us (13%)
  local copies, waits for them, and re-layouts  69.4 us (8%)
  matrix products  28.9 us (3%)
  starting transfers between devices  21.7 us (3%)
  between operations  15.7 us (2%)
  other arithmetic  10.7 us (1%)
    all_gather x7, waiting for transfers between devices, fetch_weights(): lax.all_gather(for_sending(weights), 'req', axis=0, tiled=True)  384 us
    psum x5, waiting for transfers between devices, tensor_total(): lax.psum(partial_value.astype(jnp.bfloat16), 'tp').astype(jnp.float32)  210 us
    all_gather x2, blocking collectives, fetch_weights(): lax.all_gather(for_sending(weights), 'req', axis=0, tiled=True)  108 us
    unnamed x21, local copies, waits for them, and re-layouts  42.5 us
  transfers between devices with their start and end apart: 14, of which 12 were waited for; matrix products, arithmetic and copies ran while one was open for 8% of the time, Pallas kernels for 0%

commit v1 on v0

--- a/solution.py
+++ b/solution.py
@@ -32,7 +32,9 @@
 
 
 def tensor_total(partial_value):
-    return lax.psum(partial_value.astype(jnp.bfloat16), "tp").astype(jnp.float32)
+    return jnp.sum(lax.all_gather(partial_value.astype(jnp.bfloat16), "tp"), axis=0).astype(
+        jnp.float32
+    )
 
 
 def attention(normed, w_qkv, w_out_t, allowed, sample_count):

time: 854 us -> 730 us (0.85)
  waiting for transfers between devices: 598 us -> 453 us
  blocking collectives: 108 us -> 123 us
    psum x5 -> x0, waiting for transfers between devices: 210 us -> none  [tensor_total(): lax.psum(partial_value.astype(jnp.bfloat16), 'tp').astype(jnp.float32)]
    all_gather x0 -> x4, waiting for transfers between devices: none -> 123 us  [tensor_total(): lax.all_gather(partial_value.astype(jnp.bfloat16), 'tp')]
    all_gather x7, waiting for transfers between devices: 384 us -> 325 us  [fetch_weights(): lax.all_gather(for_sending(weights), 'req', axis=0, tiled=True)]
    all_gather x0 -> x1, blocking collectives: none -> 13.9 us  [tensor_total(): lax.all_gather(partial_value.astype(jnp.bfloat16), 'tp')]
    reduce_sum x0 -> x5, other arithmetic: none -> 9.77 us  [tensor_total(): jnp.sum(lax.all_gather(partial_value.astype(jnp.bfloat16), 'tp'), axis=0)]
  transfers between devices with their start and end apart: 14 -> 13, of which waited for: 12 -> 10; matrix products, arithmetic and copies ran while one was open for 8% -> 14% of each run, Pallas kernels for 0% -> 0%
where the time goes in v1:
time: 730 us; the launch traced here: 728 us
  waiting for transfers between devices  453 us (62%)
  blocking collectives  123 us (17%)
  local copies, waits for them, and re-layouts  69.1 us (9%)
  matrix products  28.2 us (4%)
  starting transfers between devices  21.9 us (3%)
  other arithmetic  17.4 us (2%)
  between operations  15.4 us (2%)
    all_gather x7, waiting for transfers between devices, fetch_weights(): lax.all_gather(for_sending(weights), 'req', axis=0, tiled=True)  325 us
    all_gather x4, waiting for transfers between devices, tensor_total(): lax.all_gather(partial_value.astype(jnp.bfloat16), 'tp')  123 us
    all_gather x2, blocking collectives, fetch_weights(): lax.all_gather(for_sending(weights), 'req', axis=0, tiled=True)  109 us
    unnamed x21, local copies, waits for them, and re-layouts  42.6 us
    dot_general x2, matrix products, feed_forward(): lax.dot_general(hidden, w_down_t, (((1,), (1,)), ((), ())), preferred_ele...  15.7 us
  transfers between devices with their start and end apart: 13, of which 10 were waited for; matrix products, arithmetic and copies ran while one was open for 14% of the time, Pallas kernels for 0%

profile of v1, /device:TPU:8, one launch (start us, length us, event | category | flops | bytes accessed | tf_op | source)
XLA Modules:
  0.0 727.5 jit_solution(6058165702033979612)
XLA Ops:
  6.5 0.7 all-gather.34.cloned.1.call-update
  7.3 0.7 all-gather.36.cloned.1.call-update
  8.1 0.7 all-gather.38.cloned.1.call-update
  8.8 1.3 fusion.214
  11.4 53.4 %all-gather.6 = bf16[64,20,320]{2,1,0:T(8,128)(2,1)S(1)} all-gather(bf16[1,20,320]{2,1,0:T(8,128)(2,1)} %bitcast.130), channel_id=1, replica_groups=mesh['req'=64,'tp'=4] {'req'}, dimensions={0}, use_global_device_ids=true | all-gather | bytes 832000 | tf_op jit(solution)/shard_map/all_gather | solution.py:29
  64.8 0.4 reshape.284
  65.2 0.6 copy-done.1
  66.0 0.3 fusion.12
  66.4 23.8 %all-gather.34.cloned.1.call-done = bf16[64,20,960]{2,1,0:T(8,128)(2,1)} async-done(((bf16[1,20,960]{2,1,0:T(8,128)(2,1)}), bf16[64,20,960]{2,1,0:T(8,128)(2,1)}) %all-gather.34.cloned.1.call-update) | async-done | bytes 2457616 | tf_op jit(solution)/shard_map/all_gather | solution.py:29
  90.2 5.5 reshape.282
  95.7 2.9 convolution_convert_fusion.5
  98.6 0.5 fusion.215
  99.1 0.4 fusion.9
  99.5 0.4 convolution_convert_fusion.8
  99.9 1.4 convolution_convert_fusion
  101.4 0.5 all-gather.40.cloned.1.call-update
  102.1 67.1 %all-gather.36.cloned.1.call-done = bf16[64,20,1280]{2,1,0:T(8,128)(2,1)} async-done(((bf16[1,20,1280]{2,1,0:T(8,128)(2,1)}), bf16[64,20,1280]{2,1,0:T(8,128)(2,1)}) %all-gather.36.cloned.1.call-update) | async-done | bytes 3276816 | tf_op jit(solution)/shard_map/all_gather | solution.py:29
  169.2 6.1 reshape.286
  175.4 72.6 %all-gather.38.cloned.1.call-done = bf16[64,20,1280]{2,1,0:T(8,128)(2,1)} async-done(((bf16[1,20,1280]{2,1,0:T(8,128)(2,1)}), bf16[64,20,1280]{2,1,0:T(8,128)(2,1)}) %all-gather.38.cloned.1.call-update) | async-done | bytes 3276816 | tf_op jit(solution)/shard_map/all_gather | solution.py:29
  248.0 6.1 reshape.288
  254.1 31.6 %all-gather.26.cloned.1.call-done = bf16[1024,1280]{1,0:T(8,128)(2,1)} async-done(((bf16[256,1280]{1,0:T(8,128)(2,1)}), bf16[1024,1280]{1,0:T(8,128)(2,1)}) %all-gather.26.cloned.1.call-update) | async-done | bytes 2621456 | tf_op jit(solution)/shard_map/all_gather | solution.py:35
  285.7 2.4 reduce_sum.166
  288.8 8.3 %convolution_convert_fusion.1 = bf16[256,1280]{1,0:T(8,128)(2,1)} fusion(bf16[1280,1280]{1,0:T(8,128)(2,1)} %reshape.288, bf16[1280,1280]{1,0:T(8,128)(2,1)} %reshape.286, bf16[256,1280]{1,0:T(8,128)(2,1)S(1)} %get-tuple-element.8, f32[256]{0:T(256)S(1)} %add_rsqrt_fusion.2, f32[256]{0:T(256)S(1)} %broadcast_multiply_fusion.2), kind=kOutput, calls=%fused_computation.6 | convolution fusion | flops 1700659200 | bytes 7866368 | tf_op jit(solution)/shard_map/dot_general | solution.py:69
  297.2 0.7 all-gather.42.cloned.1.call-update
  297.9 0.7 all-gather.44.cloned.1.call-update
  298.7 0.7 all-gather.46.cloned.1.call-update
  299.7 1.3 and_select_fusion.2
  301.0 3.5 scatter_fusion
  304.5 0.7 copy.36
  305.2 10.6 %all-to-all-start = ((s32[64,1,2]{2,1,0:T(1,128)}), s32[64,1,2]{2,1,0:T(1,128)S(1)}, u32[]{:S(2)}, u32[]{:S(2)}) async-start(s32[64,1,2]{2,1,0:T(1,128)} %copy.36), calls=%async_computation | async-start | bytes 65536 | tf_op jit(solution)/shard_map/all_to_all | solution.py:151
  315.8 50.3 %all-gather.40.cloned.1.call-done = bf16[64,20,1280]{2,1,0:T(8,128)(2,1)} async-done(((bf16[1,20,1280]{2,1,0:T(8,128)(2,1)}), bf16[64,20,1280]{2,1,0:T(8,128)(2,1)}) %all-gather.40.cloned.1.call-update) | async-done | bytes 3276816 | tf_op jit(solution)/shard_map/all_gather | solution.py:29
  366.1 4.6 reshape.290
  370.8 33.1 %all-gather.28.cloned.1.call-done = bf16[1024,1280]{1,0:T(8,128)(2,1)} async-done(((bf16[256,1280]{1,0:T(8,128)(2,1)}), bf16[1024,1280]{1,0:T(8,128)(2,1)}) %all-gather.28.cloned.1.call-update) | async-done | bytes 2621456 | tf_op jit(solution)/shard_map/all_gather | solution.py:35
  403.9 3.2 reduce_sum.169
  407.1 2.3 fusion.15
  409.4 2.7 reshape.248
  412.0 2.4 copy.56
  414.4 2.9 reshape.249
  417.4 2.0 convolution_convert_fusion.4
  419.4 13.9 %all-gather.2 = bf16[256,1280]{1,0:T(8,128)(2,1)S(1)} all-gather(bf16[64,1280]{1,0:T(8,128)(2,1)S(1)} %convolution_convert_fusion.4), channel_id=4, replica_groups=mesh['req'=64,'tp'=4] {'tp'}, dimensions={0}, use_global_device_ids=true | all-gather | bytes 819200 | tf_op jit(solution)/shard_map/all_gather | solution.py:35
  433.4 0.9 broadcast_in_dim.47
  434.3 9.6 %scatter_fusion.1 = bf16[64,2,1280]{2,1,0:T(2,128)(2,1)} fusion(bf16[64,2,1280]{2,1,0:T(2,128)(2,1)} %broadcast_in_dim.47, s32[64]{0:T(128)S(1)} %fusion.146, bf16[64,1280]{1,0:T(8,128)(2,1)S(1)} %reduce_sum.170), kind=kCustom, calls=%fused_computation.1 | custom fusion | bytes 492032 | tf_op jit(solution)/shard_map/scatter | solution.py:142
  443.9 10.5 %all-to-all-start.1 = ((bf16[64,2,1280]{2,1,0:T(2,128)(2,1)}), bf16[64,2,1280]{2,1,0:T(2,128)(2,1)S(1)}, u32[]{:S(2)}, u32[]{:S(2)}) async-start(bf16[64,2,1280]{2,1,0:T(2,128)(2,1)} %scatter_fusion.1), calls=%async_computation.1 | async-start | bytes 655360 | tf_op jit(solution)/shard_map/all_to_all | solution.py:150
  454.5 55.6 %all-gather.11 = bf16[64,20,320]{2,1,0:T(8,128)(2,1)S(1)} all-gather(bf16[1,20,320]{2,1,0:T(8,128)(2,1)S(1)} %bitcast.131), channel_id=1, replica_groups=mesh['req'=64,'tp'=4] {'req'}, dimensions={0}, use_global_device_ids=true | all-gather | bytes 832000 | tf_op jit(solution)/shard_map/all_gather | solution.py:29
  510.0 0.4 reshape.294
  510.5 0.6 broadcast.367
  511.1 0.7 reduce.16
  511.9 5.6 reshape.292
  517.7 0.9 copy-done
  518.6 1.4 scatter_fusion.2
  520.4 2.5 convolution_convert_fusion.6
  523.1 0.5 fusion.216
  523.9 0.3 convolution_convert_fusion.7
  524.2 1.3 convolution_convert_fusion.3
  525.8 38.7 %all-gather.44.cloned.1.call-done = bf16[64,20,1280]{2,1,0:T(8,128)(2,1)} async-done(((bf16[1,20,1280]{2,1,0:T(8,128)(2,1)}), bf16[64,20,1280]{2,1,0:T(8,128)(2,1)}) %all-gather.44.cloned.1.call-update) | async-done | bytes 3276816 | tf_op jit(solution)/shard_map/all_gather | solution.py:29
  564.5 6.1 reshape.296
  570.7 72.6 %all-gather.46.cloned.1.call-done = bf16[64,20,1280]{2,1,0:T(8,128)(2,1)} async-done(((bf16[1,20,1280]{2,1,0:T(8,128)(2,1)}), bf16[64,20,1280]{2,1,0:T(8,128)(2,1)}) %all-gather.46.cloned.1.call-update) | async-done | bytes 3276816 | tf_op jit(solution)/shard_map/all_gather | solution.py:29
  643.3 6.1 reshape.298
  649.4 26.2 %all-gather.30.cloned.1.call-done = bf16[768,1280]{1,0:T(8,128)(2,1)} async-done(((bf16[192,1280]{1,0:T(8,128)(2,1)}), bf16[768,1280]{1,0:T(8,128)(2,1)}) %all-gather.30.cloned.1.call-update) | async-done | bytes 1966096 | tf_op jit(solution)/shard_map/all_gather | solution.py:35
  675.6 2.0 reduce_sum.174
  678.1 7.4 %convolution_convert_fusion.2 = bf16[192,1280]{1,0:T(8,128)(2,1)} fusion(bf16[1280,1280]{1,0:T(8,128)(2,1)} %reshape.298, bf16[1280,1280]{1,0:T(8,128)(2,1)} %reshape.296, bf16[192,1280]{1,0:T(8,128)(2,1)S(1)} %get-tuple-element.6, f32[192]{0:T(256)S(1)} %add_rsqrt_fusion, f32[192]{0:T(256)S(1)} %broadcast_multiply_fusion), kind=kOutput, calls=%fused_computation.7 | convolution fusion | flops 1275494400 | bytes 7538176 | tf_op jit(solution)/shard_map/dot_general | solution.py:69
  686.2 31.8 %all-gather.32.cloned.1.call-done = bf16[768,1280]{1,0:T(8,128)(2,1)} async-done(((bf16[192,1280]{1,0:T(8,128)(2,1)}), bf16[768,1280]{1,0:T(8,128)(2,1)}) %all-gather.32.cloned.1.call-update) | async-done | bytes 1966096 | tf_op jit(solution)/shard_map/all_gather | solution.py:35
  718.0 2.0 reduce_sum.177
  720.1 0.9 fusion.93
  (57 shorter events, 4.0 us)
Async XLA Ops:
  6.5 83.6 %all-gather.34.cloned.1.call-start = ((), (), s32[]{:S(2)}) async-start(), calls=%async_computation.6 | async-start | bytes 3194880 | tf_op jit(solution)/shard_map/all_gather | solution.py:29
  7.3 162.0 %all-gather.36.cloned.1.call-start = ((), (), s32[]{:S(2)}) async-start(), calls=%async_computation.7 | async-start | bytes 3993600 | tf_op jit(solution)/shard_map/all_gather | solution.py:29
  8.0 240.0 %all-gather.38.cloned.1.call-start = ((), (), s32[]{:S(2)}) async-start(), calls=%async_computation.8 | async-start | bytes 3993600 | tf_op jit(solution)/shard_map/all_gather | solution.py:29
  8.7 277.0 %all-gather.26.cloned.1.call-start = ((), (), s32[]{:S(2)}) async-start(), calls=%async_computation.2 | async-start | bytes 3276800 | tf_op jit(solution)/shard_map/all_gather | solution.py:35
  64.8 1.1 copy-start.1
  101.3 264.8 %all-gather.40.cloned.1.call-start = ((), (), s32[]{:S(2)}) async-start(), calls=%async_computation.9 | async-start | bytes 3993600 | tf_op jit(solution)/shard_map/all_gather | solution.py:29
  101.9 302.0 %all-gather.28.cloned.1.call-start = ((), (), s32[]{:S(2)}) async-start(), calls=%async_computation.3 | async-start | bytes 3276800 | tf_op jit(solution)/shard_map/all_gather | solution.py:35
  288.4 8.7 %copy-start.2 = (bf16[256,1280]{1,0:T(8,128)(2,1)}, bf16[256,1280]{1,0:T(8,128)(2,1)S(1)}, u32[]{:S(2)}) copy-start(bf16[256,1280]{1,0:T(8,128)(2,1)S(1)} %get-tuple-element.8) | copy-start | bytes 1966084
  288.8 10.6 %copy-start.4 = (s32[64]{0:T(128)S(1)}, s32[64]{0:T(128)}, u32[]{:S(2)}) copy-start(s32[64]{0:T(128)} %param.18) | copy-start | bytes 772
  288.8 10.9 %copy-start.5 = (s32[64]{0:T(128)S(1)}, s32[64]{0:T(128)}, u32[]{:S(2)}) copy-start(s32[64]{0:T(128)} %param.19) | copy-start | bytes 772
  297.1 214.8 %all-gather.42.cloned.1.call-start = ((), (), s32[]{:S(2)}) async-start(), calls=%async_computation.10 | async-start | bytes 3194880 | tf_op jit(solution)/shard_map/all_gather | solution.py:29
  297.9 266.7 %all-gather.44.cloned.1.call-start = ((), (), s32[]{:S(2)}) async-start(), calls=%async_computation.11 | async-start | bytes 3993600 | tf_op jit(solution)/shard_map/all_gather | solution.py:29
  298.6 344.7 %all-gather.46.cloned.1.call-start = ((), (), s32[]{:S(2)}) async-start(), calls=%async_computation.12 | async-start | bytes 3993600 | tf_op jit(solution)/shard_map/all_gather | solution.py:29
  305.2 138.7 %all-to-all-start = ((s32[64,1,2]{2,1,0:T(1,128)}), s32[64,1,2]{2,1,0:T(1,128)S(1)}, u32[]{:S(2)}, u32[]{:S(2)}) async-start(s32[64,1,2]{2,1,0:T(1,128)} %copy.36), calls=%async_computation | async-start | bytes 65536 | tf_op jit(solution)/shard_map/all_to_all | solution.py:151
  434.3 20.2 %copy-start.3 = (bf16[20,320]{1,0:T(8,128)(2,1)S(1)}, bf16[20,320]{1,0:T(8,128)(2,1)}, u32[]{:S(2)}) copy-start(bf16[20,320]{1,0:T(8,128)(2,1)} %param.27) | copy-start | bytes 38404
  443.9 73.6 %all-to-all-start.1 = ((bf16[64,2,1280]{2,1,0:T(2,128)(2,1)}), bf16[64,2,1280]{2,1,0:T(2,128)(2,1)S(1)}, u32[]{:S(2)}, u32[]{:S(2)}) async-start(bf16[64,2,1280]{2,1,0:T(2,128)(2,1)} %scatter_fusion.1), calls=%async_computation.1 | async-start | bytes 655360 | tf_op jit(solution)/shard_map/all_to_all | solution.py:150
  454.4 221.2 %all-gather.30.cloned.1.call-start = ((), (), s32[]{:S(2)}) async-start(), calls=%async_computation.4 | async-start | bytes 2457600 | tf_op jit(solution)/shard_map/all_gather | solution.py:35
  517.5 1.0 copy-start
  525.5 192.5 %all-gather.32.cloned.1.call-start = ((), (), s32[]{:S(2)}) async-start(), calls=%async_computation.5 | async-start | bytes 2457600 | tf_op jit(solution)/shard_map/all_gather | solution.py:35
Sparse Core Ops, SparseCore 0:
  10.1 80.0 all-gather.33
  92.8 76.3 all-gather.35
  171.9 76.0 all-gather.37
  249.7 36.0 all-gather.25
  288.3 77.8 all-gather.39
  367.8 36.0 all-gather.27
  406.6 78.5 all-gather.41
  487.9 76.6 all-gather.43
  567.2 76.0 all-gather.45
  644.9 30.5 all-gather.29
  685.7 32.2 all-gather.31
